TPU v7x, 32 devices: a whole 2x2x4 slice. The times are simulated.
32 devices in a mesh: inner: 8 (over y, x, core), outer: 4 (over z).
Axes of the slice: x: 2, y: 2, z: 4, core: 2. Of those that a mesh axis runs over, the one named last changes fastest.
Arguments:
- coupling: float32 [4, 8, 36, 128, 128], P('outer', 'inner'), may hold values from -0.046875 to 0.046875
- log_diag: float32 [4, 8, 1024], P('outer', 'inner'), may hold values from -0.05 to 0.05
- pattern: int32 [8, 8], replicated, may hold values 0 or 1
- boundary: float32 [1024, 256], replicated, may hold values from -6 to 6
Outputs:
- transported: float32 [4, 8, 1024, 256], P('outer', 'inner')
All inputs are finite; a program needn't handle non-finite values.
Results may differ from a plain program's by a relative error of at most 0.0003.
Values sent between devices are 32-bit elements; how exact they have to be, the bound alone decides.
A program may use at most 192 MiB of HBM per device.

v0:
```python
import functools

import jax
import jax.numpy as jnp
from jax import lax
from jax.experimental import pallas as pl
from jax.experimental.pallas import tpu as pltpu
from jax.sharding import PartitionSpec as P

MESH = pl.DeviceIdType.MESH
FIRST_FAST = 4


def split(x):
    hi = x.astype(jnp.bfloat16)
    lo = (x - hi.astype(jnp.float32)).astype(jnp.bfloat16)
    return hi, lo


def packed(i, j):
    return i * (i + 1) // 2 + j


def dot(a, b):
    return jnp.dot(a, b, preferred_element_type=jnp.float32)


def kernel(
    n_inner, total, nt, t, nc, w,
    pattern, coupling, log_diag, boundary, out,
    own, other, third, own_log, other_log, third_log, sum_log,
    lhs, rhs, scale, state, expanded, result,
    load_sem, log_sem, pair_send, pair_recv, log_send, log_recv,
    help_send, help_recv, sum_send, sum_recv,
    chain_send, chain_recv, fwd_send, beside_send, first_sem, out_sem,
):
    me = lax.axis_index("outer") * n_inner + lax.axis_index("inner")
    odd = lax.rem(me, 2) == 1
    even = jnp.logical_not(odd)
    composed = jnp.logical_and(odd, me > 1)
    spot, place = lax.rem(me, 4), me // 4
    last = total // 4 - 1

    def is_fast(index):
        return jnp.logical_and(index >= FIRST_FAST, index <= last)

    fast_pair = is_fast(place)
    slow_pair = jnp.logical_not(fast_pair)
    fast = jnp.logical_and(spot == 3, fast_pair)
    helper = jnp.logical_and(spot == 1, fast_pair)
    leaves = jnp.logical_and(spot == 3, place < last)
    beside = jnp.logical_and(spot == 2, fast_pair)
    has_next = jnp.logical_or(me == 0, jnp.logical_or(jnp.logical_and(spot == 1, slow_pair), leaves))
    step = jnp.where(spot == 1, 2, jnp.where(is_fast(place + 1), 4, 2))
    after = jnp.where(me == 0, 1, lax.rem(me + step, total))
    partner = jnp.where(odd, me - 1, me + 1)
    target = jnp.where(fast, me - 2, partner)
    before = lax.rem(me + total - jnp.where(fast, 4, 2), total)
    other_chip = jnp.where(spot == 1, me + 2, lax.rem(me + total - 2, total))
    enters = jnp.logical_or(fast, jnp.logical_and(spot == 1, jnp.logical_and(slow_pair, me > 1)))
    pair = 2 if nt % 2 == 0 else 1
    last_group = nt - pair

    def at(index):
        return {"outer": index // n_inner, "inner": lax.rem(index, n_inner)}

    def rows(i):
        return pl.ds(i * t, t)

    def load_row(i):
        part = pl.ds(packed(i, 0), i + 1)
        return pltpu.make_async_copy(coupling.at[part], own.at[part], load_sem.at[i])

    def pair_row(i):
        part = pl.ds(packed(i, 0), i + 1)
        return pltpu.make_async_remote_copy(
            src_ref=coupling.at[part], dst_ref=other.at[part],
            send_sem=pair_send.at[i], recv_sem=pair_recv.at[i],
            device_id=at(partner), device_id_type=MESH,
        )

    def pair_log():
        return pltpu.make_async_remote_copy(
            src_ref=log_diag, dst_ref=other_log,
            send_sem=log_send, recv_sem=log_recv,
            device_id=at(partner), device_id_type=MESH,
        )

    def help_rows(top):
        part = pl.ds(packed(top, 0), packed(top + pair, 0) - packed(top, 0))
        return pltpu.make_async_remote_copy(
            src_ref=own.at[part], dst_ref=third.at[part],
            send_sem=help_send.at[top // pair], recv_sem=help_recv.at[top // pair],
            device_id=at(other_chip), device_id_type=MESH,
        )

    def help_log():
        return pltpu.make_async_remote_copy(
            src_ref=sum_log, dst_ref=third_log, send_sem=sum_send, recv_sem=sum_recv,
            device_id=at(other_chip), device_id_type=MESH,
        )

    def relay_rows(top):
        part = pl.ds(packed(top, 0), packed(top + pair, 0) - packed(top, 0))
        return pltpu.make_async_remote_copy(
            src_ref=third.at[part], dst_ref=third.at[part],
            send_sem=help_send.at[top // pair], recv_sem=help_recv.at[top // pair],
            device_id=at(partner), device_id_type=MESH,
        )

    def relay_log():
        return pltpu.make_async_remote_copy(
            src_ref=third_log, dst_ref=third_log, send_sem=sum_send, recv_sem=sum_recv,
            device_id=at(partner), device_id_type=MESH,
        )

    def beside_chain(i, c):
        return pltpu.make_async_remote_copy(
            src_ref=state.at[c, rows(i)], dst_ref=state.at[c, rows(i)],
            send_sem=beside_send.at[i, c], recv_sem=chain_recv.at[i, c],
            device_id=at(partner), device_id_type=MESH,
        )

    def chain(i, c):
        return pltpu.make_async_remote_copy(
            src_ref=result.at[c, rows(i)], dst_ref=state.at[c, rows(i)],
            send_sem=chain_send.at[i, c], recv_sem=chain_recv.at[i, c],
            device_id=at(after), device_id_type=MESH,
        )

    def forward(i, c):
        return pltpu.make_async_remote_copy(
            src_ref=state.at[c, rows(i)], dst_ref=state.at[c, rows(i)],
            send_sem=fwd_send.at[i, c], recv_sem=chain_recv.at[i, c],
            device_id=at(target), device_id_type=MESH,
        )

    def first(i, c):
        return pltpu.make_async_copy(
            boundary.at[rows(i), pl.ds(c * w, w)], state.at[c, rows(i)], first_sem.at[i, c]
        )

    def store(i, c):
        return pltpu.make_async_copy(
            result.at[c, rows(i)], out.at[rows(i), pl.ds(c * w, w)], out_sem.at[i, c]
        )

    for i in range(nt):
        load_row(i).start()
    pltpu.make_async_copy(log_diag, own_log, log_sem).start()

    @pl.when(me == 0)
    def _():
        for i in range(nt):
            for c in range(nc):
                first(i, c).start()

    def weight(i, j):
        return 1.0 if i == j else pattern[i, j].astype(jnp.float32)

    def put_lhs(buf, i, j, tile):
        hi, lo = split(tile)
        buf[rows(i), pl.ds(j * 3 * t, t)] = hi
        buf[rows(i), pl.ds(j * 3 * t + t, t)] = hi
        buf[rows(i), pl.ds(j * 3 * t + 2 * t, t)] = lo

    def put_rhs(i, j, tile):
        hi, lo = split(tile)
        rhs[pl.ds(i * 3 * t, t), pl.ds(j * t, t)] = hi
        rhs[pl.ds(i * 3 * t + t, t), pl.ds(j * t, t)] = lo
        rhs[pl.ds(i * 3 * t + 2 * t, t), pl.ds(j * t, t)] = hi

    def growth(ref, i):
        return jnp.transpose(jnp.broadcast_to(jnp.exp(ref[pl.ds(i, 1), :]), (t, t)))

    def clear(buf):
        for i in range(0, nt, pair):
            for j in range(i + 1, i + pair):
                buf[rows(i), pl.ds(j * 3 * t, 3 * t)] = jnp.zeros((t, 3 * t), jnp.bfloat16)

    def prepare(i):
        scale[rows(i), :] = growth(own_log, i)
        load_row(i).wait()
        for j in range(i + 1):
            put_lhs(lhs, i, j, own[packed(i, j)] * weight(i, j))

    def multiply(buf, top, left_scale, right, keep):
        for left in range(0, top + pair, pair):
            deep = pl.ds(left * 3 * t, (top + pair - left) * 3 * t)
            block = dot(buf[pl.ds(top * t, pair * t), deep], rhs[deep, pl.ds(left * t, pair * t)])
            for a in range(pair):
                for b in range(pair):
                    r, s = top + a, left + b
                    if s <= r:
                        tile = block[a * t : (a + 1) * t, b * t : (b + 1) * t]
                        tile += left_scale[rows(r), :] * right(r, s)
                        put_lhs(buf, r, s, tile)
                        if keep:
                            own[packed(r, s)] = tile

    eye = lax.broadcasted_iota(jnp.int32, (t, t), 0) == lax.broadcasted_iota(jnp.int32, (t, t), 1)

    def clear_both():
        clear(lhs)
        for i in range(0, nt, pair):
            for j in range(i + 1, i + pair):
                rhs[pl.ds(i * 3 * t, 3 * t), pl.ds(j * t, t)] = jnp.zeros((3 * t, t), jnp.bfloat16)

    def compose_start():
        clear_both()
        pair_log().wait_recv()
        sum_log[...] = own_log[...] + other_log[...]

    def compose(top):
        for i in range(top, top + pair):
            pair_row(i).wait_recv()
            for j in range(i + 1):
                tile = other[packed(i, j)] * weight(i, j)
                if i == j:
                    grown = jnp.broadcast_to(jnp.exp(other_log[pl.ds(i, 1), :]), (t, t))
                    tile = tile + jnp.where(eye, grown, 0.0)
                put_rhs(i, j, tile)
        multiply(lhs, top, scale, lambda r, s: other[packed(r, s)] * weight(r, s), True)
        for i in range(top, top + pair):
            scale[rows(i), :] = scale[rows(i), :] * growth(other_log, i)

    def compose_fast(top):
        help_rows(top).wait_recv()

        @pl.when(fast)
        def _():
            relay_rows(top).start()

        for i in range(top, top + pair):
            grown = growth(third_log, i)
            for j in range(i + 1):
                tile = third[packed(i, j)]
                if i == j:
                    tile = tile + jnp.where(eye, grown, 0.0)
                put_rhs(i, j, tile)
        multiply(lhs, top, scale, lambda r, s: third[packed(r, s)], False)
        for i in range(top, top + pair):
            scale[rows(i), :] = scale[rows(i), :] * growth(third_log, i)

    barrier = pltpu.get_barrier_semaphore()
    pl.semaphore_signal(barrier, inc=1, device_id=at(partner), device_id_type=MESH)

    for met, whom in ((odd, other_chip), (enters, before), (leaves, after)):
        @pl.when(met)
        def _():
            pl.semaphore_signal(barrier, inc=1, device_id=at(whom), device_id_type=MESH)

    pltpu.make_async_copy(log_diag, own_log, log_sem).wait()
    prepare(0)

    greeted = 1
    for met in (odd, enters, leaves):
        greeted = greeted + met.astype(jnp.int32)
    pl.semaphore_wait(barrier, greeted)

    sends_pair = jnp.logical_and(even, me > 0)

    @pl.when(sends_pair)
    def _():
        pair_log().start()
        for i in range(nt):
            pair_row(i).start()

    @pl.when(me > 1)
    def _():
        for i in range(1, nt):
            prepare(i)

    @pl.when(composed)
    def _():
        compose_start()

        @pl.when(helper)
        def _():
            help_log().start()

    @pl.when(jnp.logical_and(composed, me != 3))
    def _():
        for top in range(0, nt, pair):
            compose(top)

            @pl.when(helper)
            def _():
                help_rows(top).start()

    @pl.when(beside)
    def _():
        clear_both()

    @pl.when(jnp.logical_or(fast, beside))
    def _():
        help_log().wait_recv()

        @pl.when(fast)
        def _():
            relay_log().start()

        for top in range(0, last_group, pair):
            compose_fast(top)

    for i in range(nt):
        if i:
            @pl.when(me < 2)
            def _():
                prepare(i)

        if i % pair == 0:
            @pl.when(me == 3)
            def _():
                compose(i)

        if i == last_group:
            @pl.when(jnp.logical_or(fast, beside))
            def _():
                compose_fast(i)

        if i:
            deep = pl.ds(0, i * 3 * t)
            partial = dot(lhs[rows(i), deep], expanded[deep, :])
            for c in range(nc):
                result[c, rows(i), :] = partial[:, c * w : (c + 1) * w]

        for c in range(nc):
            @pl.when(me == 0)
            def _():
                first(i, c).wait()

            @pl.when(me > 0)
            def _():
                chain(i, c).wait_recv()

            @pl.when(composed)
            def _():
                forward(i, c).start()

            @pl.when(fast)
            def _():
                beside_chain(i, c).start()

            x = state[c, rows(i), :]
            hi, lo = split(x)
            piece = jnp.concatenate([hi, lo, hi], axis=0)
            expanded[pl.ds(i * 3 * t, 3 * t), pl.ds(c * w, w)] = piece
            tip = pl.ds(i * 3 * t, 3 * t)
            y = dot(lhs[rows(i), tip], piece) + scale[rows(i), :w] * x
            if i:
                y += result[c, rows(i), :]
            result[c, rows(i), :] = y

            @pl.when(has_next)
            def _():
                chain(i, c).start()

            store(i, c).start()

    for i in range(nt):
        for c in range(nc):
            store(i, c).wait()

            @pl.when(has_next)
            def _():
                chain(i, c).wait_send()

            @pl.when(composed)
            def _():
                forward(i, c).wait_send()

            @pl.when(fast)
            def _():
                beside_chain(i, c).wait_send()

    @pl.when(sends_pair)
    def _():
        pair_log().wait_send()
        for i in range(nt):
            pair_row(i).wait_send()

    @pl.when(helper)
    def _():
        help_log().wait_send()
        for top in range(0, nt, pair):
            help_rows(top).wait_send()

    @pl.when(fast)
    def _():
        relay_log().wait_send()
        for top in range(0, nt, pair):
            relay_rows(top).wait_send()


def solution(mesh):
    n_inner, n_outer = mesh.shape["inner"], mesh.shape["outer"]

    def shards(coupling, log_diag, pattern, boundary):
        t = coupling.shape[-1]
        m, b = boundary.shape
        nt = m // t
        w = min(t, b)
        nc = b // w
        tiles = coupling.shape[2]
        dma = pltpu.SemaphoreType.DMA
        anywhere = pl.BlockSpec(memory_space=pl.ANY)
        result = pl.pallas_call(
            functools.partial(kernel, n_inner, n_inner * n_outer, nt, t, nc, w),
            out_shape=jax.ShapeDtypeStruct((m, b), jnp.float32),
            in_specs=[pl.BlockSpec(memory_space=pltpu.SMEM)] + [anywhere] * 3,
            out_specs=anywhere,
            scratch_shapes=[
                pltpu.VMEM((tiles, t, t), jnp.float32),
                pltpu.VMEM((tiles, t, t), jnp.float32),
                pltpu.VMEM((tiles, t, t), jnp.float32),
                pltpu.VMEM((nt, t), jnp.float32),
                pltpu.VMEM((nt, t), jnp.float32),
                pltpu.VMEM((nt, t), jnp.float32),
                pltpu.VMEM((nt, t), jnp.float32),
                pltpu.VMEM((m, 3 * m), jnp.bfloat16),
                pltpu.VMEM((3 * m, m), jnp.bfloat16),
                pltpu.VMEM((m, t), jnp.float32),
                pltpu.VMEM((nc, m, w), jnp.float32),
                pltpu.VMEM((3 * m, b), jnp.bfloat16),
                pltpu.VMEM((nc, m, w), jnp.float32),
                dma((nt,)), dma, dma((nt,)), dma((nt,)), dma, dma,
                dma((nt,)), dma((nt,)), dma, dma,
                dma((nt, nc)), dma((nt, nc)), dma((nt, nc)), dma((nt, nc)), dma((nt, nc)), dma((nt, nc)),
            ],
            compiler_params=pltpu.CompilerParams(collective_id=0, has_side_effects=True),
        )(pattern, coupling[0, 0], log_diag.reshape(nt, t), boundary)
        return result[None, None]

    return jax.shard_map(
        shards,
        mesh=mesh,
        in_specs=(P("outer", "inner", None, None, None), P("outer", "inner", None), P(), P()),
        out_specs=P("outer", "inner", None, None),
        check_vma=False,
    )
```

profile of v0, /device:TPU:29, one launch (start us, length us, event | category | flops | bytes accessed | tf_op | source)
XLA Modules:
  0.0 51.4 jit_solution(12132443721833112707)
XLA Ops:
  0.0 49.1 %shard_map.46 = f32[1024,256]{1,0:T(8,128)} custom-call(s32[8,8]{1,0:T(8,128)} %pattern.1, f32[36,128,128]{2,1,0:T(8,128)} %bitcast.4, f32[8,128]{1,0:T(8,128)} %bitcast.5, f32[1024,256]{1,0:T(8,128)} %boundary.1), custom_call_target="tpu_custom_call" | custom-call | tf_op jit(solution)/shard_map/pallas_call | solution.py:408
  49.1 2.3 %copy.6 = f32[1,1,1024,256]{3,2,1,0:T(8,128)} copy(f32[1,1,1024,256]{3,2,1,0:T(8,128)} %bitcast.3) | data formatting | bytes 2097152
where the time goes:
time: 52.1 us; the launch traced here: 51.4 us
  Pallas kernels  49.1 us (94%)
  local copies, waits for them, and re-layouts  2.26 us (4%)
    pallas_call x1, Pallas kernels, shards(): pl.pallas_call(functools.partial(kernel, n_inner, n_inner * n_outer, nt,...  49.1 us
    unnamed x1, local copies, waits for them, and re-layouts  2.26 us

commit v1 on v0

--- a/solution.py
+++ b/solution.py
@@ -8,7 +8,7 @@
 from jax.sharding import PartitionSpec as P
 
 MESH = pl.DeviceIdType.MESH
-FIRST_FAST = 4
+FIRST_FAST = 2
 
 
 def split(x):
@@ -29,10 +29,11 @@
     n_inner, total, nt, t, nc, w,
     pattern, coupling, log_diag, boundary, out,
     own, other, third, own_log, other_log, third_log, sum_log,
-    lhs, rhs, scale, state, expanded, result,
+    lhs, rhs, scale, state, expanded, result, tall, tall_scale, tall_result,
     load_sem, log_sem, pair_send, pair_recv, log_send, log_recv,
     help_send, help_recv, sum_send, sum_recv,
-    chain_send, chain_recv, fwd_send, beside_send, first_sem, out_sem,
+    lend_send, lend_log_send,
+    chain_send, twin_send, chain_recv, fwd_send, first_sem,
 ):
     me = lax.axis_index("outer") * n_inner + lax.axis_index("inner")
     odd = lax.rem(me, 2) == 1
@@ -44,20 +45,28 @@
     def is_fast(index):
         return jnp.logical_and(index >= FIRST_FAST, index <= last)
 
-    fast_pair = is_fast(place)
-    slow_pair = jnp.logical_not(fast_pair)
-    fast = jnp.logical_and(spot == 3, fast_pair)
-    helper = jnp.logical_and(spot == 1, fast_pair)
-    leaves = jnp.logical_and(spot == 3, place < last)
-    beside = jnp.logical_and(spot == 2, fast_pair)
-    has_next = jnp.logical_or(me == 0, jnp.logical_or(jnp.logical_and(spot == 1, slow_pair), leaves))
-    step = jnp.where(spot == 1, 2, jnp.where(is_fast(place + 1), 4, 2))
-    after = jnp.where(me == 0, 1, lax.rem(me + step, total))
+    here_fast, next_fast, prev_fast = is_fast(place), is_fast(place + 1), is_fast(place - 1)
+    slow = jnp.logical_not(here_fast)
+    inside = place < last
+    left, right = spot == 1, spot == 3
+    fast = jnp.logical_and(right, here_fast)
+    helper = jnp.logical_and(left, here_fast)
+    beside = jnp.logical_and(spot == 2, here_fast)
+    lends = jnp.logical_and(fast, inside)
+    adopts = jnp.logical_and(helper, inside)
+    leaves = jnp.logical_and(right, inside)
+    sends_all = jnp.logical_or(me == 0, jnp.logical_and(slow, jnp.logical_or(left, leaves)))
+    sends_low = jnp.logical_or(sends_all, leaves)
+    twin_low = jnp.logical_and(leaves, next_fast)
+    twin_all = jnp.logical_and(twin_low, slow)
+    after = jnp.where(me == 0, 1, lax.rem(me + jnp.where(helper, 4, 2), total))
+    twin = lax.rem(me + jnp.where(helper, 6, 4), total)
     partner = jnp.where(odd, me - 1, me + 1)
-    target = jnp.where(fast, me - 2, partner)
-    before = lax.rem(me + total - jnp.where(fast, 4, 2), total)
-    other_chip = jnp.where(spot == 1, me + 2, lax.rem(me + total - 2, total))
-    enters = jnp.logical_or(fast, jnp.logical_and(spot == 1, jnp.logical_and(slow_pair, me > 1)))
+    other_chip = jnp.where(left, me + 2, lax.rem(me + total - 2, total))
+    back_right = lax.rem(me + total - jnp.where(left, 2, 4), total)
+    back_left = lax.rem(me + total - jnp.where(left, 4, 6), total)
+    enters = jnp.logical_or(fast, jnp.logical_and(left, me > 1))
+    enters_two = jnp.logical_and(jnp.logical_and(odd, here_fast), prev_fast)
     pair = 2 if nt % 2 == 0 else 1
     last_group = nt - pair
 
@@ -114,11 +123,18 @@
             device_id=at(partner), device_id_type=MESH,
         )
 
-    def beside_chain(i, c):
-        return pltpu.make_async_remote_copy(
-            src_ref=state.at[c, rows(i)], dst_ref=state.at[c, rows(i)],
-            send_sem=beside_send.at[i, c], recv_sem=chain_recv.at[i, c],
-            device_id=at(partner), device_id_type=MESH,
+    def lend_rows():
+        part = pl.ds(packed(last_group, 0), packed(nt, 0) - packed(last_group, 0))
+        return pltpu.make_async_remote_copy(
+            src_ref=own.at[part], dst_ref=third.at[part],
+            send_sem=lend_send, recv_sem=help_recv.at[last_group // pair],
+            device_id=at(other_chip), device_id_type=MESH,
+        )
+
+    def lend_log():
+        return pltpu.make_async_remote_copy(
+            src_ref=sum_log, dst_ref=third_log, send_sem=lend_log_send, recv_sem=sum_recv,
+            device_id=at(other_chip), device_id_type=MESH,
         )
 
     def chain(i, c):
@@ -128,21 +144,37 @@
             device_id=at(after), device_id_type=MESH,
         )
 
+    def chain_twin(i, c):
+        return pltpu.make_async_remote_copy(
+            src_ref=result.at[c, rows(i)], dst_ref=state.at[c, rows(i)],
+            send_sem=twin_send.at[i, c], recv_sem=chain_recv.at[i, c],
+            device_id=at(twin), device_id_type=MESH,
+        )
+
+    def tall_chain(i, c):
+        return pltpu.make_async_remote_copy(
+            src_ref=tall_result.at[c, rows(i - last_group)], dst_ref=state.at[c, rows(i)],
+            send_sem=chain_send.at[i, c], recv_sem=chain_recv.at[i, c],
+            device_id=at(after), device_id_type=MESH,
+        )
+
+    def tall_twin(i, c):
+        return pltpu.make_async_remote_copy(
+            src_ref=tall_result.at[c, rows(i - last_group)], dst_ref=state.at[c, rows(i)],
+            send_sem=twin_send.at[i, c], recv_sem=chain_recv.at[i, c],
+            device_id=at(twin), device_id_type=MESH,
+        )
+
     def forward(i, c):
         return pltpu.make_async_remote_copy(
             src_ref=state.at[c, rows(i)], dst_ref=state.at[c, rows(i)],
             send_sem=fwd_send.at[i, c], recv_sem=chain_recv.at[i, c],
-            device_id=at(target), device_id_type=MESH,
+            device_id=at(partner), device_id_type=MESH,
         )
 
     def first(i, c):
         return pltpu.make_async_copy(
             boundary.at[rows(i), pl.ds(c * w, w)], state.at[c, rows(i)], first_sem.at[i, c]
-        )
-
-    def store(i, c):
-        return pltpu.make_async_copy(
-            result.at[c, rows(i)], out.at[rows(i), pl.ds(c * w, w)], out_sem.at[i, c]
         )
 
     for i in range(nt):
@@ -184,17 +216,17 @@
         for j in range(i + 1):
             put_lhs(lhs, i, j, own[packed(i, j)] * weight(i, j))
 
-    def multiply(buf, top, left_scale, right, keep):
+    def multiply(buf, top, left_scale, right, keep, base=0):
         for left in range(0, top + pair, pair):
             deep = pl.ds(left * 3 * t, (top + pair - left) * 3 * t)
-            block = dot(buf[pl.ds(top * t, pair * t), deep], rhs[deep, pl.ds(left * t, pair * t)])
+            block = dot(buf[pl.ds((top - base) * t, pair * t), deep], rhs[deep, pl.ds(left * t, pair * t)])
             for a in range(pair):
                 for b in range(pair):
                     r, s = top + a, left + b
                     if s <= r:
                         tile = block[a * t : (a + 1) * t, b * t : (b + 1) * t]
-                        tile += left_scale[rows(r), :] * right(r, s)
-                        put_lhs(buf, r, s, tile)
+                        tile += left_scale[rows(r - base), :] * right(r, s)
+                        put_lhs(buf, r - base, s, tile)
                         if keep:
                             own[packed(r, s)] = tile
 
@@ -211,7 +243,7 @@
         pair_log().wait_recv()
         sum_log[...] = own_log[...] + other_log[...]
 
-    def compose(top):
+    def compose_take(top):
         for i in range(top, top + pair):
             pair_row(i).wait_recv()
             for j in range(i + 1):
@@ -220,9 +252,37 @@
                     grown = jnp.broadcast_to(jnp.exp(other_log[pl.ds(i, 1), :]), (t, t))
                     tile = tile + jnp.where(eye, grown, 0.0)
                 put_rhs(i, j, tile)
+
+    def compose_make(top):
         multiply(lhs, top, scale, lambda r, s: other[packed(r, s)] * weight(r, s), True)
         for i in range(top, top + pair):
             scale[rows(i), :] = scale[rows(i), :] * growth(other_log, i)
+
+    def compose(top):
+        compose_take(top)
+        compose_make(top)
+
+    def adopt_start():
+        for i in range(nt):
+            for j in range(i + 1):
+                tile = own[packed(i, j)]
+                if i == j:
+                    tile = tile + jnp.where(eye, scale[rows(i), :], 0.0)
+                put_rhs(i, j, tile)
+
+    def adopt():
+        help_rows(last_group).wait_recv()
+        for a in range(pair):
+            r = last_group + a
+            tall_scale[rows(a), :] = growth(third_log, r)
+            for j in range(nt):
+                if j <= r:
+                    put_lhs(tall, a, j, third[packed(r, j)])
+                else:
+                    tall[rows(a), pl.ds(j * 3 * t, 3 * t)] = jnp.zeros((t, 3 * t), jnp.bfloat16)
+        multiply(tall, last_group, tall_scale, lambda r, s: own[packed(r, s)], False, last_group)
+        for a in range(pair):
+            tall_scale[rows(a), :] = tall_scale[rows(a), :] * scale[rows(last_group + a), :]
 
     def compose_fast(top):
         help_rows(top).wait_recv()
@@ -245,18 +305,18 @@
     barrier = pltpu.get_barrier_semaphore()
     pl.semaphore_signal(barrier, inc=1, device_id=at(partner), device_id_type=MESH)
 
-    for met, whom in ((odd, other_chip), (enters, before), (leaves, after)):
+    for met, whom in (
+        (jnp.logical_or(right, adopts), other_chip), (enters, back_right), (enters_two, back_left)
+    ):
         @pl.when(met)
         def _():
             pl.semaphore_signal(barrier, inc=1, device_id=at(whom), device_id_type=MESH)
 
     pltpu.make_async_copy(log_diag, own_log, log_sem).wait()
-    prepare(0)
-
-    greeted = 1
-    for met in (odd, enters, leaves):
-        greeted = greeted + met.astype(jnp.int32)
-    pl.semaphore_wait(barrier, greeted)
+
+    @pl.when(even)
+    def _():
+        pl.semaphore_wait(barrier, 1)
 
     sends_pair = jnp.logical_and(even, me > 0)
 
@@ -266,6 +326,8 @@
         for i in range(nt):
             pair_row(i).start()
 
+    prepare(0)
+
     @pl.when(me > 1)
     def _():
         for i in range(1, nt):
@@ -275,18 +337,44 @@
     def _():
         compose_start()
 
+    greeted = 1
+    for met in (left, lends, leaves, twin_low, adopts, adopts):
+        greeted = greeted + met.astype(jnp.int32)
+
+    @pl.when(odd)
+    def _():
+        pl.semaphore_wait(barrier, greeted)
+
+    @pl.when(jnp.logical_and(left, me > 1))
+    def _():
         @pl.when(helper)
         def _():
             help_log().start()
 
-    @pl.when(jnp.logical_and(composed, me != 3))
-    def _():
         for top in range(0, nt, pair):
             compose(top)
 
             @pl.when(helper)
             def _():
                 help_rows(top).start()
+
+        @pl.when(adopts)
+        def _():
+            adopt_start()
+
+    @pl.when(jnp.logical_and(right, me != 3))
+    def _():
+        for top in range(0, nt, pair):
+            compose_take(top)
+        compose_make(last_group)
+
+        @pl.when(lends)
+        def _():
+            lend_log().start()
+            lend_rows().start()
+
+        for top in range(0, last_group, pair):
+            compose_make(top)
 
     @pl.when(beside)
     def _():
@@ -300,7 +388,7 @@
         def _():
             relay_log().start()
 
-        for top in range(0, last_group, pair):
+        for top in range(0, max(last_group - pair, 0), pair):
             compose_fast(top)
 
     for i in range(nt):
@@ -314,10 +402,24 @@
             def _():
                 compose(i)
 
-        if i == last_group:
+        if i == last_group or i == last_group - pair:
             @pl.when(jnp.logical_or(fast, beside))
             def _():
                 compose_fast(i)
+
+        if i == max(last_group - 1, 0):
+            @pl.when(adopts)
+            def _():
+                help_log().wait_recv()
+                adopt()
+
+        if i >= last_group and i:
+            @pl.when(adopts)
+            def _():
+                deep = pl.ds(0, i * 3 * t)
+                partial = dot(tall[rows(i - last_group), deep], expanded[deep, :])
+                for c in range(nc):
+                    tall_result[c, rows(i - last_group), :] = partial[:, c * w : (c + 1) * w]
 
         if i:
             deep = pl.ds(0, i * 3 * t)
@@ -338,41 +440,56 @@
             def _():
                 forward(i, c).start()
 
-            @pl.when(fast)
-            def _():
-                beside_chain(i, c).start()
-
             x = state[c, rows(i), :]
             hi, lo = split(x)
             piece = jnp.concatenate([hi, lo, hi], axis=0)
             expanded[pl.ds(i * 3 * t, 3 * t), pl.ds(c * w, w)] = piece
             tip = pl.ds(i * 3 * t, 3 * t)
+            if i >= last_group:
+                @pl.when(adopts)
+                def _():
+                    a = i - last_group
+                    y = dot(tall[rows(a), tip], piece) + tall_scale[rows(a), :w] * x
+                    if i:
+                        y += tall_result[c, rows(a), :]
+                    tall_result[c, rows(a), :] = y
+                    tall_chain(i, c).start()
+                    tall_twin(i, c).start()
+
             y = dot(lhs[rows(i), tip], piece) + scale[rows(i), :w] * x
             if i:
                 y += result[c, rows(i), :]
             result[c, rows(i), :] = y
 
-            @pl.when(has_next)
+            @pl.when(sends_low if i < last_group else sends_all)
             def _():
                 chain(i, c).start()
 
-            store(i, c).start()
+            @pl.when(twin_low if i < last_group else twin_all)
+            def _():
+                chain_twin(i, c).start()
+
+            out[rows(i), pl.ds(c * w, w)] = y
 
     for i in range(nt):
         for c in range(nc):
-            store(i, c).wait()
-
-            @pl.when(has_next)
+            @pl.when(sends_low if i < last_group else sends_all)
             def _():
                 chain(i, c).wait_send()
 
+            @pl.when(twin_low if i < last_group else twin_all)
+            def _():
+                chain_twin(i, c).wait_send()
+
+            if i >= last_group:
+                @pl.when(adopts)
+                def _():
+                    tall_chain(i, c).wait_send()
+                    tall_twin(i, c).wait_send()
+
             @pl.when(composed)
             def _():
                 forward(i, c).wait_send()
-
-            @pl.when(fast)
-            def _():
-                beside_chain(i, c).wait_send()
 
     @pl.when(sends_pair)
     def _():
@@ -385,6 +502,11 @@
         help_log().wait_send()
         for top in range(0, nt, pair):
             help_rows(top).wait_send()
+
+    @pl.when(lends)
+    def _():
+        lend_log().wait_send()
+        lend_rows().wait_send()
 
     @pl.when(fast)
     def _():
@@ -402,14 +524,15 @@
         nt = m // t
         w = min(t, b)
         nc = b // w
+        pair = 2 if nt % 2 == 0 else 1
         tiles = coupling.shape[2]
         dma = pltpu.SemaphoreType.DMA
         anywhere = pl.BlockSpec(memory_space=pl.ANY)
         result = pl.pallas_call(
             functools.partial(kernel, n_inner, n_inner * n_outer, nt, t, nc, w),
-            out_shape=jax.ShapeDtypeStruct((m, b), jnp.float32),
+            out_shape=pltpu.VMEM((m, b), jnp.float32),
             in_specs=[pl.BlockSpec(memory_space=pltpu.SMEM)] + [anywhere] * 3,
-            out_specs=anywhere,
+            out_specs=pl.BlockSpec(memory_space=pltpu.VMEM),
             scratch_shapes=[
                 pltpu.VMEM((tiles, t, t), jnp.float32),
                 pltpu.VMEM((tiles, t, t), jnp.float32),
@@ -424,9 +547,13 @@
                 pltpu.VMEM((nc, m, w), jnp.float32),
                 pltpu.VMEM((3 * m, b), jnp.bfloat16),
                 pltpu.VMEM((nc, m, w), jnp.float32),
+                pltpu.VMEM((pair * t, 3 * m), jnp.bfloat16),
+                pltpu.VMEM((pair * t, t), jnp.float32),
+                pltpu.VMEM((nc, pair * t, w), jnp.float32),
                 dma((nt,)), dma, dma((nt,)), dma((nt,)), dma, dma,
                 dma((nt,)), dma((nt,)), dma, dma,
-                dma((nt, nc)), dma((nt, nc)), dma((nt, nc)), dma((nt, nc)), dma((nt, nc)), dma((nt, nc)),
+                dma, dma,
+                dma((nt, nc)), dma((nt, nc)), dma((nt, nc)), dma((nt, nc)), dma((nt, nc)),
             ],
             compiler_params=pltpu.CompilerParams(collective_id=0, has_side_effects=True),
         )(pattern, coupling[0, 0], log_diag.reshape(nt, t), boundary)

time: 52.1 us -> 52 us (level)
  Pallas kernels: 49.1 us -> 50.8 us
  local copies, waits for them, and re-layouts: 2.26 us -> 0.97 us
    pallas_call x1, Pallas kernels: 49.1 us -> 50.8 us  [shards(): pl.pallas_call(functools.partial(kernel, n_inner, n_inner * n_outer, nt,...]
    unnamed x1, local copies, waits for them, and re-layouts: 2.26 us -> 0.97 us
where the time goes in v1:
time: 52 us; the launch traced here: 51.8 us
  Pallas kernels  50.8 us (98%)
  local copies, waits for them, and re-layouts  0.97 us (2%)
    pallas_call x1, Pallas kernels, shards(): pl.pallas_call(functools.partial(kernel, n_inner, n_inner * n_outer, nt,...  50.8 us

profile of v1, /device:TPU:29, one launch (start us, length us, event | category | flops | bytes accessed | tf_op | source)
XLA Modules:
  0.0 51.8 jit_solution(2688568066748986325)
XLA Ops:
  0.0 50.8 %shard_map.46 = f32[1024,256]{1,0:T(8,128)S(1)} custom-call(s32[8,8]{1,0:T(8,128)} %pattern.1, f32[36,128,128]{2,1,0:T(8,128)} %bitcast.4, f32[8,128]{1,0:T(8,128)} %bitcast.5, f32[1024,256]{1,0:T(8,128)} %boundary.1), custom_call_target="tpu_custom_call" | custom-call | tf_op jit(solution)/shard_map/pallas_call | solution.py:531
  50.8 1.0 %copy.6 = f32[1,1,1024,256]{3,2,1,0:T(8,128)} copy(f32[1,1,1024,256]{3,2,1,0:T(8,128)S(1)} %bitcast.3) | data formatting | bytes 2097152

commit v2 on v1

--- a/solution.py
+++ b/solution.py
@@ -33,7 +33,7 @@
     load_sem, log_sem, pair_send, pair_recv, log_send, log_recv,
     help_send, help_recv, sum_send, sum_recv,
     lend_send, lend_log_send,
-    chain_send, twin_send, chain_recv, fwd_send, first_sem,
+    chain_send, twin_send, relay_send, chain_recv, fwd_send, first_sem,
 ):
     me = lax.axis_index("outer") * n_inner + lax.axis_index("inner")
     odd = lax.rem(me, 2) == 1
@@ -55,18 +55,22 @@
     lends = jnp.logical_and(fast, inside)
     adopts = jnp.logical_and(helper, inside)
     leaves = jnp.logical_and(right, inside)
+    turns = lax.rem(place, 2) == 1
+    direct = jnp.logical_and(prev_fast, turns)
+    hands = jnp.logical_and(helper, jnp.logical_not(direct))
+    twins = jnp.logical_and(adopts, jnp.logical_not(turns))
     sends_all = jnp.logical_or(me == 0, jnp.logical_and(slow, jnp.logical_or(left, leaves)))
     sends_low = jnp.logical_or(sends_all, leaves)
-    twin_low = jnp.logical_and(leaves, next_fast)
-    twin_all = jnp.logical_and(twin_low, slow)
-    after = jnp.where(me == 0, 1, lax.rem(me + jnp.where(helper, 4, 2), total))
-    twin = lax.rem(me + jnp.where(helper, 6, 4), total)
+    splits = jnp.logical_and(leaves, next_fast)
+    after_low = jnp.where(me == 0, 1, lax.rem(me + jnp.where(splits, 4, 2), total))
+    after_high = jnp.where(me == 0, 1, lax.rem(me + jnp.where(helper, 4, 2), total))
+    twin = lax.rem(me + 6, total)
     partner = jnp.where(odd, me - 1, me + 1)
     other_chip = jnp.where(left, me + 2, lax.rem(me + total - 2, total))
-    back_right = lax.rem(me + total - jnp.where(left, 2, 4), total)
-    back_left = lax.rem(me + total - jnp.where(left, 4, 6), total)
     enters = jnp.logical_or(fast, jnp.logical_and(left, me > 1))
-    enters_two = jnp.logical_and(jnp.logical_and(odd, here_fast), prev_fast)
+    back = lax.rem(me + total - jnp.where(jnp.logical_or(fast, jnp.logical_and(left, prev_fast)), 4, 2), total)
+    enters_two = jnp.logical_and(fast, direct)
+    back_left = lax.rem(me + total - 6, total)
     pair = 2 if nt % 2 == 0 else 1
     last_group = nt - pair
 
@@ -141,21 +145,21 @@
         return pltpu.make_async_remote_copy(
             src_ref=result.at[c, rows(i)], dst_ref=state.at[c, rows(i)],
             send_sem=chain_send.at[i, c], recv_sem=chain_recv.at[i, c],
-            device_id=at(after), device_id_type=MESH,
-        )
-
-    def chain_twin(i, c):
-        return pltpu.make_async_remote_copy(
-            src_ref=result.at[c, rows(i)], dst_ref=state.at[c, rows(i)],
-            send_sem=twin_send.at[i, c], recv_sem=chain_recv.at[i, c],
-            device_id=at(twin), device_id_type=MESH,
+            device_id=at(after_low if i < last_group else after_high), device_id_type=MESH,
+        )
+
+    def relay(i, c):
+        return pltpu.make_async_remote_copy(
+            src_ref=state.at[c, rows(i)], dst_ref=state.at[c, rows(i)],
+            send_sem=relay_send.at[i, c], recv_sem=chain_recv.at[i, c],
+            device_id=at(other_chip), device_id_type=MESH,
         )
 
     def tall_chain(i, c):
         return pltpu.make_async_remote_copy(
             src_ref=tall_result.at[c, rows(i - last_group)], dst_ref=state.at[c, rows(i)],
             send_sem=chain_send.at[i, c], recv_sem=chain_recv.at[i, c],
-            device_id=at(after), device_id_type=MESH,
+            device_id=at(after_high), device_id_type=MESH,
         )
 
     def tall_twin(i, c):
@@ -306,7 +310,7 @@
     pl.semaphore_signal(barrier, inc=1, device_id=at(partner), device_id_type=MESH)
 
     for met, whom in (
-        (jnp.logical_or(right, adopts), other_chip), (enters, back_right), (enters_two, back_left)
+        (jnp.logical_or(right, helper), other_chip), (enters, back), (enters_two, back_left)
     ):
         @pl.when(met)
         def _():
@@ -338,7 +342,7 @@
         compose_start()
 
     greeted = 1
-    for met in (left, lends, leaves, twin_low, adopts, adopts):
+    for met in (left, fast, leaves, jnp.logical_and(splits, slow), adopts, twins):
         greeted = greeted + met.astype(jnp.int32)
 
     @pl.when(odd)
@@ -435,6 +439,10 @@
             @pl.when(me > 0)
             def _():
                 chain(i, c).wait_recv()
+
+            @pl.when(fast if i < last_group else hands)
+            def _():
+                relay(i, c).start()
 
             @pl.when(composed)
             def _():
@@ -454,7 +462,10 @@
                         y += tall_result[c, rows(a), :]
                     tall_result[c, rows(a), :] = y
                     tall_chain(i, c).start()
-                    tall_twin(i, c).start()
+
+                    @pl.when(twins)
+                    def _():
+                        tall_twin(i, c).start()
 
             y = dot(lhs[rows(i), tip], piece) + scale[rows(i), :w] * x
             if i:
@@ -465,10 +476,6 @@
             def _():
                 chain(i, c).start()
 
-            @pl.when(twin_low if i < last_group else twin_all)
-            def _():
-                chain_twin(i, c).start()
-
             out[rows(i), pl.ds(c * w, w)] = y
 
     for i in range(nt):
@@ -477,14 +484,17 @@
             def _():
                 chain(i, c).wait_send()
 
-            @pl.when(twin_low if i < last_group else twin_all)
-            def _():
-                chain_twin(i, c).wait_send()
+            @pl.when(fast if i < last_group else hands)
+            def _():
+                relay(i, c).wait_send()
 
             if i >= last_group:
                 @pl.when(adopts)
                 def _():
                     tall_chain(i, c).wait_send()
+
+                @pl.when(twins)
+                def _():
                     tall_twin(i, c).wait_send()
 
             @pl.when(composed)
@@ -553,7 +563,7 @@
                 dma((nt,)), dma, dma((nt,)), dma((nt,)), dma, dma,
                 dma((nt,)), dma((nt,)), dma, dma,
                 dma, dma,
-                dma((nt, nc)), dma((nt, nc)), dma((nt, nc)), dma((nt, nc)), dma((nt, nc)),
+                dma((nt, nc)), dma((nt, nc)), dma((nt, nc)), dma((nt, nc)), dma((nt, nc)), dma((nt, nc)),
             ],
             compiler_params=pltpu.CompilerParams(collective_id=0, has_side_effects=True),
         )(pattern, coupling[0, 0], log_diag.reshape(nt, t), boundary)

time: 52 us -> 52.1 us (level)
  the two profiles are of different devices: /device:TPU:29 before, /device:TPU:31 now
where the time goes in v2:
time: 52.1 us; the launch traced here: 51.9 us
  Pallas kernels  50.9 us (98%)
  local copies, waits for them, and re-layouts  0.97 us (2%)
    pallas_call x1, Pallas kernels, shards(): pl.pallas_call(functools.partial(kernel, n_inner, n_inner * n_outer, nt,...  50.9 us

profile of v2, /device:TPU:31, one launch (start us, length us, event | category | flops | bytes accessed | tf_op | source)
XLA Modules:
  0.0 51.9 jit_solution(13741769141304563748)
XLA Ops:
  0.0 50.9 %shard_map.46 = f32[1024,256]{1,0:T(8,128)S(1)} custom-call(s32[8,8]{1,0:T(8,128)} %pattern.1, f32[36,128,128]{2,1,0:T(8,128)} %bitcast.4, f32[8,128]{1,0:T(8,128)} %bitcast.5, f32[1024,256]{1,0:T(8,128)} %boundary.1), custom_call_target="tpu_custom_call" | custom-call | tf_op jit(solution)/shard_map/pallas_call | solution.py:541
  50.9 1.0 %copy.6 = f32[1,1,1024,256]{3,2,1,0:T(8,128)} copy(f32[1,1,1024,256]{3,2,1,0:T(8,128)S(1)} %bitcast.3) | data formatting | bytes 2097152

commit v3 on v2

--- a/solution.py
+++ b/solution.py
@@ -8,7 +8,7 @@
 from jax.sharding import PartitionSpec as P
 
 MESH = pl.DeviceIdType.MESH
-FIRST_FAST = 2
+FIRST_FAST = 3
 
 
 def split(x):
@@ -27,13 +27,14 @@
 
 def kernel(
     n_inner, total, nt, t, nc, w,
-    pattern, coupling, log_diag, boundary, out,
+    pattern_hbm, coupling, log_diag, boundary, out,
+    pattern, pattern_sem,
     own, other, third, own_log, other_log, third_log, sum_log,
     lhs, rhs, scale, state, expanded, result, tall, tall_scale, tall_result,
     load_sem, log_sem, pair_send, pair_recv, log_send, log_recv,
     help_send, help_recv, sum_send, sum_recv,
     lend_send, lend_log_send,
-    chain_send, twin_send, relay_send, chain_recv, fwd_send, first_sem,
+    chain_send, left_send, relay_send, chain_recv, fwd_send, first_sem,
 ):
     me = lax.axis_index("outer") * n_inner + lax.axis_index("inner")
     odd = lax.rem(me, 2) == 1
@@ -55,24 +56,20 @@
     lends = jnp.logical_and(fast, inside)
     adopts = jnp.logical_and(helper, inside)
     leaves = jnp.logical_and(right, inside)
-    turns = lax.rem(place, 2) == 1
-    direct = jnp.logical_and(prev_fast, turns)
-    hands = jnp.logical_and(helper, jnp.logical_not(direct))
-    twins = jnp.logical_and(adopts, jnp.logical_not(turns))
-    sends_all = jnp.logical_or(me == 0, jnp.logical_and(slow, jnp.logical_or(left, leaves)))
-    sends_low = jnp.logical_or(sends_all, leaves)
-    splits = jnp.logical_and(leaves, next_fast)
-    after_low = jnp.where(me == 0, 1, lax.rem(me + jnp.where(splits, 4, 2), total))
-    after_high = jnp.where(me == 0, 1, lax.rem(me + jnp.where(helper, 4, 2), total))
-    twin = lax.rem(me + 6, total)
+    relays = jnp.logical_and(fast, prev_fast)
+    splits = jnp.logical_and(jnp.logical_and(leaves, slow), next_fast)
+    sends_all = jnp.logical_or(
+        me == 0, jnp.logical_or(leaves, jnp.logical_and(left, slow))
+    )
+    after = jnp.where(me == 0, 1, lax.rem(me + jnp.where(jnp.logical_and(leaves, next_fast), 4, 2), total))
+    after_left = lax.rem(me + jnp.where(left, 4, 2), total)
     partner = jnp.where(odd, me - 1, me + 1)
     other_chip = jnp.where(left, me + 2, lax.rem(me + total - 2, total))
     enters = jnp.logical_or(fast, jnp.logical_and(left, me > 1))
     back = lax.rem(me + total - jnp.where(jnp.logical_or(fast, jnp.logical_and(left, prev_fast)), 4, 2), total)
-    enters_two = jnp.logical_and(fast, direct)
-    back_left = lax.rem(me + total - 6, total)
     pair = 2 if nt % 2 == 0 else 1
     last_group = nt - pair
+    defer = max(last_group - 1, 0)
 
     def at(index):
         return {"outer": index // n_inner, "inner": lax.rem(index, n_inner)}
@@ -145,7 +142,14 @@
         return pltpu.make_async_remote_copy(
             src_ref=result.at[c, rows(i)], dst_ref=state.at[c, rows(i)],
             send_sem=chain_send.at[i, c], recv_sem=chain_recv.at[i, c],
-            device_id=at(after_low if i < last_group else after_high), device_id_type=MESH,
+            device_id=at(after), device_id_type=MESH,
+        )
+
+    def chain_left(i, c):
+        return pltpu.make_async_remote_copy(
+            src_ref=result.at[c, rows(i)], dst_ref=state.at[c, rows(i)],
+            send_sem=left_send.at[i, c], recv_sem=chain_recv.at[i, c],
+            device_id=at(after_left), device_id_type=MESH,
         )
 
     def relay(i, c):
@@ -158,15 +162,8 @@
     def tall_chain(i, c):
         return pltpu.make_async_remote_copy(
             src_ref=tall_result.at[c, rows(i - last_group)], dst_ref=state.at[c, rows(i)],
-            send_sem=chain_send.at[i, c], recv_sem=chain_recv.at[i, c],
-            device_id=at(after_high), device_id_type=MESH,
-        )
-
-    def tall_twin(i, c):
-        return pltpu.make_async_remote_copy(
-            src_ref=tall_result.at[c, rows(i - last_group)], dst_ref=state.at[c, rows(i)],
-            send_sem=twin_send.at[i, c], recv_sem=chain_recv.at[i, c],
-            device_id=at(twin), device_id_type=MESH,
+            send_sem=left_send.at[i, c], recv_sem=chain_recv.at[i, c],
+            device_id=at(after_left), device_id_type=MESH,
         )
 
     def forward(i, c):
@@ -181,15 +178,6 @@
             boundary.at[rows(i), pl.ds(c * w, w)], state.at[c, rows(i)], first_sem.at[i, c]
         )
 
-    for i in range(nt):
-        load_row(i).start()
-    pltpu.make_async_copy(log_diag, own_log, log_sem).start()
-
-    @pl.when(me == 0)
-    def _():
-        for i in range(nt):
-            for c in range(nc):
-                first(i, c).start()
 
     def weight(i, j):
         return 1.0 if i == j else pattern[i, j].astype(jnp.float32)
@@ -310,13 +298,32 @@
     pl.semaphore_signal(barrier, inc=1, device_id=at(partner), device_id_type=MESH)
 
     for met, whom in (
-        (jnp.logical_or(right, helper), other_chip), (enters, back), (enters_two, back_left)
+        (jnp.logical_or(right, adopts), other_chip), (enters, back)
     ):
         @pl.when(met)
         def _():
             pl.semaphore_signal(barrier, inc=1, device_id=at(whom), device_id_type=MESH)
 
-    pltpu.make_async_copy(log_diag, own_log, log_sem).wait()
+    pltpu.make_async_copy(pattern_hbm, pattern, pattern_sem).start()
+    pltpu.make_async_copy(log_diag, own_log, log_sem).start()
+
+    @pl.when(me < 2)
+    def _():
+        load_row(0).start()
+
+    @pl.when(me == 0)
+    def _():
+        for c in range(nc):
+            first(0, c).start()
+
+    @pl.when(odd)
+    def _():
+        @pl.when(me > 1)
+        def _():
+            load_row(0).start()
+
+        for i in range(1, nt):
+            load_row(i).start()
 
     @pl.when(even)
     def _():
@@ -330,6 +337,22 @@
         for i in range(nt):
             pair_row(i).start()
 
+    @pl.when(even)
+    def _():
+        @pl.when(me > 0)
+        def _():
+            load_row(0).start()
+
+        for i in range(1, nt):
+            load_row(i).start()
+
+            @pl.when(me == 0)
+            def _():
+                for c in range(nc):
+                    first(i, c).start()
+
+    pltpu.make_async_copy(log_diag, own_log, log_sem).wait()
+    pltpu.make_async_copy(pattern_hbm, pattern, pattern_sem).wait()
     prepare(0)
 
     @pl.when(me > 1)
@@ -342,7 +365,7 @@
         compose_start()
 
     greeted = 1
-    for met in (left, fast, leaves, jnp.logical_and(splits, slow), adopts, twins):
+    for met in (left, lends, leaves, splits, adopts):
         greeted = greeted + met.astype(jnp.int32)
 
     @pl.when(odd)
@@ -411,26 +434,30 @@
             def _():
                 compose_fast(i)
 
-        if i == max(last_group - 1, 0):
+        if i == defer:
             @pl.when(adopts)
             def _():
                 help_log().wait_recv()
                 adopt()
-
-        if i >= last_group and i:
-            @pl.when(adopts)
-            def _():
-                deep = pl.ds(0, i * 3 * t)
-                partial = dot(tall[rows(i - last_group), deep], expanded[deep, :])
-                for c in range(nc):
-                    tall_result[c, rows(i - last_group), :] = partial[:, c * w : (c + 1) * w]
-
-        if i:
+                if i:
+                    deep = pl.ds(0, i * 3 * t)
+                    partial = dot(tall[:, deep], expanded[deep, :])
+                    for c in range(nc):
+                        tall_result[c] = partial[:, c * w : (c + 1) * w]
+                else:
+                    tall_result[...] = jnp.zeros_like(tall_result)
+
+        def gather(i=i):
             deep = pl.ds(0, i * 3 * t)
             partial = dot(lhs[rows(i), deep], expanded[deep, :])
             for c in range(nc):
                 result[c, rows(i), :] = partial[:, c * w : (c + 1) * w]
 
+        if 0 < i < defer:
+            gather()
+        elif i:
+            pl.when(jnp.logical_not(adopts))(gather)
+
         for c in range(nc):
             @pl.when(me == 0)
             def _():
@@ -440,9 +467,10 @@
             def _():
                 chain(i, c).wait_recv()
 
-            @pl.when(fast if i < last_group else hands)
-            def _():
-                relay(i, c).start()
+            if i < last_group:
+                @pl.when(relays)
+                def _():
+                    relay(i, c).start()
 
             @pl.when(composed)
             def _():
@@ -453,49 +481,67 @@
             piece = jnp.concatenate([hi, lo, hi], axis=0)
             expanded[pl.ds(i * 3 * t, 3 * t), pl.ds(c * w, w)] = piece
             tip = pl.ds(i * 3 * t, 3 * t)
-            if i >= last_group:
+            if i >= defer:
                 @pl.when(adopts)
                 def _():
-                    a = i - last_group
-                    y = dot(tall[rows(a), tip], piece) + tall_scale[rows(a), :w] * x
-                    if i:
-                        y += tall_result[c, rows(a), :]
-                    tall_result[c, rows(a), :] = y
-                    tall_chain(i, c).start()
-
-                    @pl.when(twins)
-                    def _():
-                        tall_twin(i, c).start()
-
-            y = dot(lhs[rows(i), tip], piece) + scale[rows(i), :w] * x
-            if i:
-                y += result[c, rows(i), :]
-            result[c, rows(i), :] = y
-
-            @pl.when(sends_low if i < last_group else sends_all)
-            def _():
-                chain(i, c).start()
-
-            out[rows(i), pl.ds(c * w, w)] = y
+                    a = max(i - last_group, 0)
+                    low = pl.ds(a * t, (pair - a) * t)
+                    y = dot(tall[low, tip], piece) + tall_result[c, low, :]
+                    if i >= last_group:
+                        top = y[:t] + tall_scale[rows(a), :w] * x
+                        y = top if a + 1 == pair else jnp.concatenate([top, y[t:]], axis=0)
+                    tall_result[c, low, :] = y
+                    if i >= last_group:
+                        tall_chain(i, c).start()
+
+            def finish(i=i, c=c, x=x, piece=piece, tip=tip):
+                y = dot(lhs[rows(i), tip], piece) + scale[rows(i), :w] * x
+                if i:
+                    y += result[c, rows(i), :]
+                result[c, rows(i), :] = y
+
+                @pl.when(sends_all)
+                def _():
+                    chain(i, c).start()
+
+                @pl.when(splits)
+                def _():
+                    chain_left(i, c).start()
+
+                out[rows(i), pl.ds(c * w, w)] = y
+
+            if i < defer:
+                finish()
+            else:
+                pl.when(jnp.logical_not(adopts))(finish)
+
+    @pl.when(adopts)
+    def _():
+        for i in range(defer, nt):
+            deep = pl.ds(0, (i + 1) * 3 * t)
+            y = dot(lhs[rows(i), deep], expanded[deep, :])
+            for c in range(nc):
+                part = pl.ds(c * w, w)
+                out[rows(i), part] = y[:, c * w : (c + 1) * w] + scale[rows(i), :w] * state[c, rows(i), :]
 
     for i in range(nt):
         for c in range(nc):
-            @pl.when(sends_low if i < last_group else sends_all)
+            @pl.when(sends_all)
             def _():
                 chain(i, c).wait_send()
 
-            @pl.when(fast if i < last_group else hands)
-            def _():
-                relay(i, c).wait_send()
-
-            if i >= last_group:
+            @pl.when(splits)
+            def _():
+                chain_left(i, c).wait_send()
+
+            if i < last_group:
+                @pl.when(relays)
+                def _():
+                    relay(i, c).wait_send()
+            else:
                 @pl.when(adopts)
                 def _():
                     tall_chain(i, c).wait_send()
-
-                @pl.when(twins)
-                def _():
-                    tall_twin(i, c).wait_send()
 
             @pl.when(composed)
             def _():
@@ -541,9 +587,11 @@
         result = pl.pallas_call(
             functools.partial(kernel, n_inner, n_inner * n_outer, nt, t, nc, w),
             out_shape=pltpu.VMEM((m, b), jnp.float32),
-            in_specs=[pl.BlockSpec(memory_space=pltpu.SMEM)] + [anywhere] * 3,
+            in_specs=[anywhere] * 4,
             out_specs=pl.BlockSpec(memory_space=pltpu.VMEM),
             scratch_shapes=[
+                pltpu.SMEM(pattern.shape, jnp.int32),
+                dma,
                 pltpu.VMEM((tiles, t, t), jnp.float32),
                 pltpu.VMEM((tiles, t, t), jnp.float32),
                 pltpu.VMEM((tiles, t, t), jnp.float32),

time: 52.1 us -> 48.2 us (0.925)
  the two profiles are of different devices: /device:TPU:31 before, /device:TPU:29 now
where the time goes in v3:
time: 48.2 us; the launch traced here: 48 us
  Pallas kernels  47.1 us (98%)
  local copies, waits for them, and re-layouts  0.97 us (2%)
    pallas_call x1, Pallas kernels, shards(): pl.pallas_call(functools.partial(kernel, n_inner, n_inner * n_outer, nt,...  47.1 us
    unnamed x1, local copies, waits for them, and re-layouts  0.97 us

profile of v3, /device:TPU:29, one launch (start us, length us, event | category | flops | bytes accessed | tf_op | source)
XLA Modules:
  0.0 48.0 jit_solution(12247743522411376529)
XLA Ops:
  0.0 47.1 %shard_map.46 = f32[1024,256]{1,0:T(8,128)S(1)} custom-call(s32[8,8]{1,0:T(8,128)} %pattern_hbm.1, f32[36,128,128]{2,1,0:T(8,128)} %bitcast.4, f32[8,128]{1,0:T(8,128)} %bitcast.5, f32[1024,256]{1,0:T(8,128)} %boundary.1), custom_call_target="tpu_custom_call" | custom-call | tf_op jit(solution)/shard_map/pallas_call | solution.py:587
  47.1 1.0 %copy.6 = f32[1,1,1024,256]{3,2,1,0:T(8,128)} copy(f32[1,1,1024,256]{3,2,1,0:T(8,128)S(1)} %bitcast.3) | data formatting | bytes 2097152

commit v4 on v3

--- a/solution.py
+++ b/solution.py
@@ -70,6 +70,13 @@
     pair = 2 if nt % 2 == 0 else 1
     last_group = nt - pair
     defer = max(last_group - 1, 0)
+    groups = [(top, pair) for top in range(0, last_group, pair)] + [(top, 1) for top in range(last_group, nt)]
+    tail = [g for g, (top, _) in enumerate(groups) if top >= last_group]
+    head = [g for g in range(len(groups)) if g not in tail]
+
+    def span(g):
+        top, n = groups[g]
+        return pl.ds(packed(top, 0), packed(top + n, 0) - packed(top, 0))
 
     def at(index):
         return {"outer": index // n_inner, "inner": lax.rem(index, n_inner)}
@@ -96,11 +103,11 @@
             device_id=at(partner), device_id_type=MESH,
         )
 
-    def help_rows(top):
-        part = pl.ds(packed(top, 0), packed(top + pair, 0) - packed(top, 0))
+    def help_rows(g):
+        part = span(g)
         return pltpu.make_async_remote_copy(
             src_ref=own.at[part], dst_ref=third.at[part],
-            send_sem=help_send.at[top // pair], recv_sem=help_recv.at[top // pair],
+            send_sem=help_send.at[g], recv_sem=help_recv.at[g],
             device_id=at(other_chip), device_id_type=MESH,
         )
 
@@ -110,11 +117,11 @@
             device_id=at(other_chip), device_id_type=MESH,
         )
 
-    def relay_rows(top):
-        part = pl.ds(packed(top, 0), packed(top + pair, 0) - packed(top, 0))
+    def relay_rows(g):
+        part = span(g)
         return pltpu.make_async_remote_copy(
             src_ref=third.at[part], dst_ref=third.at[part],
-            send_sem=help_send.at[top // pair], recv_sem=help_recv.at[top // pair],
+            send_sem=help_send.at[g], recv_sem=help_recv.at[g],
             device_id=at(partner), device_id_type=MESH,
         )
 
@@ -124,11 +131,11 @@
             device_id=at(partner), device_id_type=MESH,
         )
 
-    def lend_rows():
-        part = pl.ds(packed(last_group, 0), packed(nt, 0) - packed(last_group, 0))
+    def lend_rows(g):
+        part = span(g)
         return pltpu.make_async_remote_copy(
             src_ref=own.at[part], dst_ref=third.at[part],
-            send_sem=lend_send, recv_sem=help_recv.at[last_group // pair],
+            send_sem=lend_send.at[g], recv_sem=help_recv.at[g],
             device_id=at(other_chip), device_id_type=MESH,
         )
 
@@ -208,11 +215,12 @@
         for j in range(i + 1):
             put_lhs(lhs, i, j, own[packed(i, j)] * weight(i, j))
 
-    def multiply(buf, top, left_scale, right, keep, base=0):
-        for left in range(0, top + pair, pair):
-            deep = pl.ds(left * 3 * t, (top + pair - left) * 3 * t)
-            block = dot(buf[pl.ds((top - base) * t, pair * t), deep], rhs[deep, pl.ds(left * t, pair * t)])
-            for a in range(pair):
+    def multiply(buf, g, left_scale, right, keep, base=0):
+        top, n = groups[g]
+        for left in range(0, top + n, pair):
+            deep = pl.ds(left * 3 * t, (top + n - left) * 3 * t)
+            block = dot(buf[pl.ds((top - base) * t, n * t), deep], rhs[deep, pl.ds(left * t, pair * t)])
+            for a in range(n):
                 for b in range(pair):
                     r, s = top + a, left + b
                     if s <= r:
@@ -235,8 +243,12 @@
         pair_log().wait_recv()
         sum_log[...] = own_log[...] + other_log[...]
 
-    def compose_take(top):
-        for i in range(top, top + pair):
+    def members(g):
+        top, n = groups[g]
+        return range(top, top + n)
+
+    def compose_take(g):
+        for i in members(g):
             pair_row(i).wait_recv()
             for j in range(i + 1):
                 tile = other[packed(i, j)] * weight(i, j)
@@ -245,14 +257,14 @@
                     tile = tile + jnp.where(eye, grown, 0.0)
                 put_rhs(i, j, tile)
 
-    def compose_make(top):
-        multiply(lhs, top, scale, lambda r, s: other[packed(r, s)] * weight(r, s), True)
-        for i in range(top, top + pair):
+    def compose_make(g):
+        multiply(lhs, g, scale, lambda r, s: other[packed(r, s)] * weight(r, s), True)
+        for i in members(g):
             scale[rows(i), :] = scale[rows(i), :] * growth(other_log, i)
 
-    def compose(top):
-        compose_take(top)
-        compose_make(top)
+    def compose(g):
+        compose_take(g)
+        compose_make(g)
 
     def adopt_start():
         for i in range(nt):
@@ -263,35 +275,34 @@
                 put_rhs(i, j, tile)
 
     def adopt():
-        help_rows(last_group).wait_recv()
-        for a in range(pair):
+        for a, g in enumerate(tail):
             r = last_group + a
+            help_rows(g).wait_recv()
             tall_scale[rows(a), :] = growth(third_log, r)
             for j in range(nt):
                 if j <= r:
                     put_lhs(tall, a, j, third[packed(r, j)])
                 else:
                     tall[rows(a), pl.ds(j * 3 * t, 3 * t)] = jnp.zeros((t, 3 * t), jnp.bfloat16)
-        multiply(tall, last_group, tall_scale, lambda r, s: own[packed(r, s)], False, last_group)
-        for a in range(pair):
-            tall_scale[rows(a), :] = tall_scale[rows(a), :] * scale[rows(last_group + a), :]
-
-    def compose_fast(top):
-        help_rows(top).wait_recv()
+            multiply(tall, g, tall_scale, lambda r, s: own[packed(r, s)], False, last_group)
+            tall_scale[rows(a), :] = tall_scale[rows(a), :] * scale[rows(r), :]
+
+    def compose_fast(g):
+        help_rows(g).wait_recv()
 
         @pl.when(fast)
         def _():
-            relay_rows(top).start()
-
-        for i in range(top, top + pair):
+            relay_rows(g).start()
+
+        for i in members(g):
             grown = growth(third_log, i)
             for j in range(i + 1):
                 tile = third[packed(i, j)]
                 if i == j:
                     tile = tile + jnp.where(eye, grown, 0.0)
                 put_rhs(i, j, tile)
-        multiply(lhs, top, scale, lambda r, s: third[packed(r, s)], False)
-        for i in range(top, top + pair):
+        multiply(lhs, g, scale, lambda r, s: third[packed(r, s)], False)
+        for i in members(g):
             scale[rows(i), :] = scale[rows(i), :] * growth(third_log, i)
 
     barrier = pltpu.get_barrier_semaphore()
@@ -355,7 +366,7 @@
     pltpu.make_async_copy(pattern_hbm, pattern, pattern_sem).wait()
     prepare(0)
 
-    @pl.when(me > 1)
+    @pl.when(jnp.logical_or(jnp.logical_and(even, me > 1), me == 3))
     def _():
         for i in range(1, nt):
             prepare(i)
@@ -378,12 +389,15 @@
         def _():
             help_log().start()
 
-        for top in range(0, nt, pair):
-            compose(top)
+        for g in range(len(groups)):
+            for i in members(g):
+                if i:
+                    prepare(i)
+            compose(g)
 
             @pl.when(helper)
             def _():
-                help_rows(top).start()
+                help_rows(g).start()
 
         @pl.when(adopts)
         def _():
@@ -391,17 +405,28 @@
 
     @pl.when(jnp.logical_and(right, me != 3))
     def _():
-        for top in range(0, nt, pair):
-            compose_take(top)
-        compose_make(last_group)
+        for i in range(last_group, nt):
+            if i:
+                prepare(i)
+        for g in range(len(groups)):
+            compose_take(g)
 
         @pl.when(lends)
         def _():
             lend_log().start()
-            lend_rows().start()
-
-        for top in range(0, last_group, pair):
-            compose_make(top)
+
+        for g in tail:
+            compose_make(g)
+
+            @pl.when(lends)
+            def _():
+                lend_rows(g).start()
+
+        for g in head:
+            for i in members(g):
+                if i:
+                    prepare(i)
+            compose_make(g)
 
     @pl.when(beside)
     def _():
@@ -415,8 +440,8 @@
         def _():
             relay_log().start()
 
-        for top in range(0, max(last_group - pair, 0), pair):
-            compose_fast(top)
+        for g in head[:-1]:
+            compose_fast(g)
 
     for i in range(nt):
         if i:
@@ -424,15 +449,16 @@
             def _():
                 prepare(i)
 
-        if i % pair == 0:
-            @pl.when(me == 3)
-            def _():
-                compose(i)
-
-        if i == last_group or i == last_group - pair:
-            @pl.when(jnp.logical_or(fast, beside))
-            def _():
-                compose_fast(i)
+        for g in range(len(groups)):
+            if groups[g][0] == i:
+                @pl.when(me == 3)
+                def _():
+                    compose(g)
+
+                if g in tail or g in head[-1:]:
+                    @pl.when(jnp.logical_or(fast, beside))
+                    def _():
+                        compose_fast(g)
 
         if i == defer:
             @pl.when(adopts)
@@ -556,19 +582,20 @@
     @pl.when(helper)
     def _():
         help_log().wait_send()
-        for top in range(0, nt, pair):
-            help_rows(top).wait_send()
+        for g in range(len(groups)):
+            help_rows(g).wait_send()
 
     @pl.when(lends)
     def _():
         lend_log().wait_send()
-        lend_rows().wait_send()
+        for g in tail:
+            lend_rows(g).wait_send()
 
     @pl.when(fast)
     def _():
         relay_log().wait_send()
-        for top in range(0, nt, pair):
-            relay_rows(top).wait_send()
+        for g in range(len(groups)):
+            relay_rows(g).wait_send()
 
 
 def solution(mesh):
@@ -610,7 +637,7 @@
                 pltpu.VMEM((nc, pair * t, w), jnp.float32),
                 dma((nt,)), dma, dma((nt,)), dma((nt,)), dma, dma,
                 dma((nt,)), dma((nt,)), dma, dma,
-                dma, dma,
+                dma((nt,)), dma,
                 dma((nt, nc)), dma((nt, nc)), dma((nt, nc)), dma((nt, nc)), dma((nt, nc)), dma((nt, nc)),
             ],
             compiler_params=pltpu.CompilerParams(collective_id=0, has_side_effects=True),

time: 48.2 us -> 46.9 us (0.973)
  Pallas kernels: 47.1 us -> 45.8 us
    pallas_call x1, Pallas kernels: 47.1 us -> 45.8 us  [shards(): pl.pallas_call(functools.partial(kernel, n_inner, n_inner * n_outer, nt,...]
where the time goes in v4:
time: 46.9 us; the launch traced here: 46.8 us
  Pallas kernels  45.8 us (98%)
  local copies, waits for them, and re-layouts  0.97 us (2%)
    pallas_call x1, Pallas kernels, shards(): pl.pallas_call(functools.partial(kernel, n_inner, n_inner * n_outer, nt,...  45.8 us
    unnamed x1, local copies, waits for them, and re-layouts  0.97 us

profile of v4, /device:TPU:29, one launch (start us, length us, event | category | flops | bytes accessed | tf_op | source)
XLA Modules:
  0.0 46.8 jit_solution(14412510248179699755)
XLA Ops:
  0.0 45.8 %shard_map.46 = f32[1024,256]{1,0:T(8,128)S(1)} custom-call(s32[8,8]{1,0:T(8,128)} %pattern_hbm.1, f32[36,128,128]{2,1,0:T(8,128)} %bitcast.4, f32[8,128]{1,0:T(8,128)} %bitcast.5, f32[1024,256]{1,0:T(8,128)} %boundary.1), custom_call_target="tpu_custom_call" | custom-call | tf_op jit(solution)/shard_map/pallas_call | solution.py:614
  45.8 1.0 %copy.6 = f32[1,1,1024,256]{3,2,1,0:T(8,128)} copy(f32[1,1,1024,256]{3,2,1,0:T(8,128)S(1)} %bitcast.3) | data formatting | bytes 2097152

commit v5 on v4

--- a/solution.py
+++ b/solution.py
@@ -61,6 +61,8 @@
     sends_all = jnp.logical_or(
         me == 0, jnp.logical_or(leaves, jnp.logical_and(left, slow))
     )
+    firsts = jnp.logical_and(lends, jnp.logical_not(prev_fast))
+    ferries = jnp.logical_and(splits, place + 1 < last)
     after = jnp.where(me == 0, 1, lax.rem(me + jnp.where(jnp.logical_and(leaves, next_fast), 4, 2), total))
     after_left = lax.rem(me + jnp.where(left, 4, 2), total)
     partner = jnp.where(odd, me - 1, me + 1)
@@ -137,6 +139,25 @@
             src_ref=own.at[part], dst_ref=third.at[part],
             send_sem=lend_send.at[g], recv_sem=help_recv.at[g],
             device_id=at(other_chip), device_id_type=MESH,
+        )
+
+    def piece_of(k):
+        first_tile = packed(last_group, 0)
+        half = (last_group + 2) // 2
+        return pl.ds(first_tile + k * half, half if k == 0 else last_group + 1 - half)
+
+    def ferry_in(k):
+        return pltpu.make_async_remote_copy(
+            src_ref=own.at[piece_of(k)], dst_ref=third.at[piece_of(k)],
+            send_sem=lend_send.at[k * nt + tail[0] * (1 - k)], recv_sem=help_recv.at[k * nt + tail[0] * (1 - k)],
+            device_id=at(lax.rem(me + total - 4, total)), device_id_type=MESH,
+        )
+
+    def ferry_out(k):
+        return pltpu.make_async_remote_copy(
+            src_ref=third.at[piece_of(k)], dst_ref=third.at[piece_of(k)],
+            send_sem=help_send.at[k * nt + tail[0] * (1 - k)], recv_sem=help_recv.at[tail[0]],
+            device_id=at(after_left), device_id_type=MESH,
         )
 
     def lend_log():
@@ -309,7 +330,8 @@
     pl.semaphore_signal(barrier, inc=1, device_id=at(partner), device_id_type=MESH)
 
     for met, whom in (
-        (jnp.logical_or(right, adopts), other_chip), (enters, back)
+        (jnp.logical_or(right, adopts), other_chip), (enters, back),
+        (ferries, lax.rem(me + 4, total)),
     ):
         @pl.when(met)
         def _():
@@ -376,7 +398,7 @@
         compose_start()
 
     greeted = 1
-    for met in (left, lends, leaves, splits, adopts):
+    for met in (left, lends, leaves, splits, adopts, firsts):
         greeted = greeted + met.astype(jnp.int32)
 
     @pl.when(odd)
@@ -418,9 +440,15 @@
         for g in tail:
             compose_make(g)
 
-            @pl.when(lends)
+            @pl.when(jnp.logical_and(lends, jnp.logical_not(firsts)) if g == tail[0] else lends)
             def _():
                 lend_rows(g).start()
+
+            if g == tail[0]:
+                @pl.when(firsts)
+                def _():
+                    for k in range(2):
+                        ferry_in(k).start()
 
         for g in head:
             for i in members(g):
@@ -442,6 +470,12 @@
 
         for g in head[:-1]:
             compose_fast(g)
+
+    @pl.when(ferries)
+    def _():
+        for k in range(2):
+            ferry_in(k).wait_recv()
+            ferry_out(k).start()
 
     for i in range(nt):
         if i:
@@ -588,8 +622,22 @@
     @pl.when(lends)
     def _():
         lend_log().wait_send()
-        for g in tail:
+        for g in tail[1:]:
             lend_rows(g).wait_send()
+
+        @pl.when(firsts)
+        def _():
+            for k in range(2):
+                ferry_in(k).wait_send()
+
+        @pl.when(jnp.logical_not(firsts))
+        def _():
+            lend_rows(tail[0]).wait_send()
+
+    @pl.when(ferries)
+    def _():
+        for k in range(2):
+            ferry_out(k).wait_send()
 
     @pl.when(fast)
     def _():
@@ -636,8 +684,8 @@
                 pltpu.VMEM((pair * t, t), jnp.float32),
                 pltpu.VMEM((nc, pair * t, w), jnp.float32),
                 dma((nt,)), dma, dma((nt,)), dma((nt,)), dma, dma,
-                dma((nt,)), dma((nt,)), dma, dma,
-                dma((nt,)), dma,
+                dma((nt + 1,)), dma((nt + 1,)), dma, dma,
+                dma((nt + 1,)), dma,
                 dma((nt, nc)), dma((nt, nc)), dma((nt, nc)), dma((nt, nc)), dma((nt, nc)), dma((nt, nc)),
             ],
             compiler_params=pltpu.CompilerParams(collective_id=0, has_side_effects=True),

time: 46.9 us -> 45 us (0.959)
  Pallas kernels: 45.8 us -> 43.9 us
    pallas_call x1, Pallas kernels: 45.8 us -> 43.9 us  [shards(): pl.pallas_call(functools.partial(kernel, n_inner, n_inner * n_outer, nt,...]
where the time goes in v5:
time: 45 us; the launch traced here: 44.9 us
  Pallas kernels  43.9 us (98%)
  local copies, waits for them, and re-layouts  0.97 us (2%)
    pallas_call x1, Pallas kernels, shards(): pl.pallas_call(functools.partial(kernel, n_inner, n_inner * n_outer, nt,...  43.9 us
    unnamed x1, local copies, waits for them, and re-layouts  0.97 us

profile of v5, /device:TPU:29, one launch (start us, length us, event | category | flops | bytes accessed | tf_op | source)
XLA Modules:
  0.0 44.9 jit_solution(14260757872090696754)
XLA Ops:
  0.0 43.9 %shard_map.46 = f32[1024,256]{1,0:T(8,128)S(1)} custom-call(s32[8,8]{1,0:T(8,128)} %pattern_hbm.1, f32[36,128,128]{2,1,0:T(8,128)} %bitcast.4, f32[8,128]{1,0:T(8,128)} %bitcast.5, f32[1024,256]{1,0:T(8,128)} %boundary.1), custom_call_target="tpu_custom_call" | custom-call | tf_op jit(solution)/shard_map/pallas_call | solution.py:662
  43.9 1.0 %copy.6 = f32[1,1,1024,256]{3,2,1,0:T(8,128)} copy(f32[1,1,1024,256]{3,2,1,0:T(8,128)S(1)} %bitcast.3) | data formatting | bytes 2097152

commit v6 on v5

--- a/solution.py
+++ b/solution.py
@@ -471,6 +471,11 @@
         for g in head[:-1]:
             compose_fast(g)
 
+    @pl.when(jnp.logical_and(adopts, prev_fast))
+    def _():
+        help_log().wait_recv()
+        adopt()
+
     @pl.when(ferries)
     def _():
         for k in range(2):
@@ -494,11 +499,15 @@
                     def _():
                         compose_fast(g)
 
+        if i == max(defer - 2, 0):
+            @pl.when(jnp.logical_and(adopts, jnp.logical_not(prev_fast)))
+            def _():
+                help_log().wait_recv()
+                adopt()
+
         if i == defer:
             @pl.when(adopts)
             def _():
-                help_log().wait_recv()
-                adopt()
                 if i:
                     deep = pl.ds(0, i * 3 * t)
                     partial = dot(tall[:, deep], expanded[deep, :])

time: 45 us -> 44.5 us (0.989)
  Pallas kernels: 43.9 us -> 43.4 us
    pallas_call x1, Pallas kernels: 43.9 us -> 43.4 us  [shards(): pl.pallas_call(functools.partial(kernel, n_inner, n_inner * n_outer, nt,...]
where the time goes in v6:
time: 44.5 us; the launch traced here: 44.4 us
  Pallas kernels  43.4 us (98%)
  local copies, waits for them, and re-layouts  0.97 us (2%)
    pallas_call x1, Pallas kernels, shards(): pl.pallas_call(functools.partial(kernel, n_inner, n_inner * n_outer, nt,...  43.4 us
    unnamed x1, local copies, waits for them, and re-layouts  0.97 us

profile of v6, /device:TPU:29, one launch (start us, length us, event | category | flops | bytes accessed | tf_op | source)
XLA Modules:
  0.0 44.4 jit_solution(9030375273144815507)
XLA Ops:
  0.0 43.4 %shard_map.46 = f32[1024,256]{1,0:T(8,128)S(1)} custom-call(s32[8,8]{1,0:T(8,128)} %pattern_hbm.1, f32[36,128,128]{2,1,0:T(8,128)} %bitcast.4, f32[8,128]{1,0:T(8,128)} %bitcast.5, f32[1024,256]{1,0:T(8,128)} %boundary.1), custom_call_target="tpu_custom_call" | custom-call | tf_op jit(solution)/shard_map/pallas_call | solution.py:671
  43.4 1.0 %copy.6 = f32[1,1,1024,256]{3,2,1,0:T(8,128)} copy(f32[1,1,1024,256]{3,2,1,0:T(8,128)S(1)} %bitcast.3) | data formatting | bytes 2097152
